TPU v7x, 128 devices: a whole 4x4x4 slice. The times are simulated.
128 devices in a mesh: heads: 8 (over z, core), tok: 16 (over y, x).
Axes of the slice: x: 4, y: 4, z: 4, core: 2. Of those that a mesh axis runs over, the one named last changes fastest.
Arguments:
- states: bfloat16 [512, 7168], P('heads', 'tok'), may hold values from -10 to 10
- key_values: bfloat16 [2, 2, 8192, 7168], P(None, None, 'tok', 'heads')
- cache_length: int32 [2], replicated, may hold values from 0 to 7936, as said below
- norm1_gain: float32 [7168], replicated, may hold values from 0.25 to 1.75
- norm1_bias: float32 [7168], replicated, may hold values from -3 to 3
- qkv_weight: bfloat16 [7168, 3, 7168], P('tok', None, 'heads'), may hold values from -0.0625 to 0.0625
- qkv_bias: float32 [3, 7168], P(None, 'heads'), may hold values from -3 to 3
- out_weight: bfloat16 [7168, 7168], P('heads', 'tok'), may hold values from -0.0625 to 0.0625
- out_bias: float32 [7168], P('tok'), may hold values from -3 to 3
- norm2_gain: float32 [7168], replicated, may hold values from 0.25 to 1.75
- norm2_bias: float32 [7168], replicated, may hold values from -3 to 3
- fc1_weight: bfloat16 [7168, 28672], P(None, ('heads', 'tok')), may hold values from -0.0625 to 0.0625
- fc1_bias: float32 [28672], P(('heads', 'tok')), may hold values from -3 to 3
- fc2_weight: bfloat16 [28672, 7168], P(('heads', 'tok')), may hold values from -0.03125 to 0.03125
- fc2_bias: float32 [7168], P('tok'), may hold values from -3 to 3
Outputs:
- hidden_out: bfloat16 [512, 7168], P('heads', 'tok')
- cache_out: bfloat16 [2, 2, 8192, 7168], P(None, None, 'tok', 'heads')
Inputs may be any that keep to these rules, and one draw needn't show every extreme that they name: Request r's new tokens take positions cache_length[r] to cache_length[r] + 255 of its cache; some request reaches the largest length.
All inputs are finite; a program needn't handle non-finite values.
Results may differ from a plain program's by a relative error of at most 0.013.
The roundings to bfloat16 on the way count: a program that leaves them out, or rounds other values in their place, can miss the bound.
Values may be sent and summed in bfloat16 or wider, within the bound.
A program may use at most 192 MiB of HBM per device.

v0:
```python
import jax
import jax.numpy as jnp
from jax import lax
from jax.sharding import PartitionSpec as P

HD = 128
SINK = 4
REQS = 2
NEW = 256


EPSILON = 1e-05
NEGATIVE = -1e30


def joined(value, axis, join):
    pieces = jax.tree.map(lambda part: lax.all_gather(part, axis), value)
    head = jax.tree.map(lambda part: part[0], pieces)
    tail = jax.tree.map(lambda part: part[1:], pieces)
    so_far, _ = lax.scan(lambda so_far, section: (join(so_far, section), None), head, tail)
    return so_far


def norm_rows(values, total_sum, total_square, width, gain, shift):
    mean_row = total_sum / width
    variance = total_square / width - mean_row * mean_row
    return (
        (values - mean_row[:, None]) * lax.rsqrt(variance[:, None] + EPSILON) * gain + shift
    ).astype(jnp.bfloat16)


def merge_parts(first, second):
    highest = jnp.maximum(first[1], second[1])
    left_factor = jnp.exp(first[1] - highest)
    right_factor = jnp.exp(second[1] - highest)
    return (
        first[0] * left_factor[..., None] + second[0] * right_factor[..., None],
        highest,
        first[2] * left_factor + second[2] * right_factor,
    )


def shards(
    states,
    key_values,
    cache_length,
    norm1_gain,
    norm1_bias,
    qkv_weight,
    qkv_bias,
    out_weight,
    out_bias,
    norm2_gain,
    norm2_bias,
    fc1_weight,
    fc1_bias,
    fc2_weight,
    fc2_bias,
):
    head_count = lax.axis_size("heads")
    tok_count = lax.axis_size("tok")
    tok_index = lax.axis_index("tok")
    rows_local, cols_local = states.shape
    width = cols_local * tok_count
    group = qkv_weight.shape[2]
    group_heads = group // HD
    tokens = rows_local * head_count
    cache_rows = key_values.shape[2]
    window = cache_rows * tok_count // 2
    col_start = tok_index * cols_local
    states_float = states.astype(jnp.float32)
    row_sum, row_square = lax.psum(
        (jnp.sum(states_float, axis=1), jnp.sum(states_float * states_float, axis=1)), "tok"
    )
    gain_one = lax.dynamic_slice_in_dim(norm1_gain, col_start, cols_local)
    shift_one = lax.dynamic_slice_in_dim(norm1_bias, col_start, cols_local)
    normed_one = norm_rows(states_float, row_sum, row_square, width, gain_one, shift_one)
    gathered = lax.all_gather(normed_one, "heads", axis=0, tiled=True)
    weight_flat = qkv_weight.reshape(cols_local, 3 * group)
    factors = jnp.asarray([HD ** (-0.5), 1.0, 1.0], dtype=jnp.float32)[None, :, None]
    partial_qkv = jnp.dot(gathered, weight_flat, preferred_element_type=jnp.float32)
    summed = lax.psum(partial_qkv, "tok")
    projected = ((summed.reshape(tokens, 3, group) + qkv_bias[None]) * factors).astype(jnp.bfloat16)
    queries = projected[:, 0].reshape(REQS, NEW, group_heads, HD)
    fresh = jnp.moveaxis(projected[:, 1:].reshape(REQS, NEW, 2, group), 2, 0)
    key_pos = tok_index * cache_rows + jnp.arange(cache_rows, dtype=jnp.int32)
    appended_parts = []
    for request in range(REQS):
        offset = key_pos - cache_length[request]
        inside = (offset >= 0) & (offset < NEW)
        picked = jnp.take(fresh[:, request], jnp.clip(offset, 0, NEW - 1), axis=1)
        appended_parts.append(jnp.where(inside[None, :, None], picked, key_values[:, request]))
    appended = jnp.stack(appended_parts, axis=1)
    keys = appended[0].reshape(REQS, cache_rows, group_heads, HD)
    values = appended[1].reshape(REQS, cache_rows, group_heads, HD)
    query_pos = cache_length[:, None] + jnp.arange(NEW, dtype=jnp.int32)[None, :]
    distance = query_pos[:, :, None] - key_pos[None, None, :]
    allowed = (distance >= 0) & ((key_pos[None, None, :] < SINK) | (distance < window))
    scores = jnp.einsum("rshd,rphd->rshp", queries, keys, preferred_element_type=jnp.float32)
    masked = jnp.where(allowed[:, :, None, :], scores, NEGATIVE)
    peak = jnp.max(masked, axis=-1)
    weights = jnp.where(allowed[:, :, None, :], jnp.exp(masked - peak[..., None]), 0.0)
    totals = jnp.sum(weights, axis=-1)
    partial_out = jnp.einsum(
        "rshp,rphd->rshd", weights.astype(jnp.bfloat16), values, preferred_element_type=jnp.float32
    )
    merged, highest, denominator = joined((partial_out, peak, totals), "tok", merge_parts)
    attended = (merged / denominator[..., None]).astype(jnp.bfloat16).reshape(tokens, group)
    projected_out = lax.psum_scatter(
        jnp.dot(attended, out_weight, preferred_element_type=jnp.float32),
        "heads",
        scatter_dimension=0,
        tiled=True,
    )
    residual = (states_float + projected_out + out_bias).astype(jnp.bfloat16)
    residual_float = residual.astype(jnp.float32)
    second_sum, second_square = lax.psum(
        (jnp.sum(residual_float, axis=1), jnp.sum(residual_float * residual_float, axis=1)), "tok"
    )
    gain_two = lax.dynamic_slice_in_dim(norm2_gain, col_start, cols_local)
    shift_two = lax.dynamic_slice_in_dim(norm2_bias, col_start, cols_local)
    normed_part = norm_rows(residual_float, second_sum, second_square, width, gain_two, shift_two)
    normed = lax.all_gather(normed_part, "tok", axis=1, tiled=True)
    active = jnp.maximum(
        jnp.dot(
            lax.all_gather(normed, "heads", axis=0, tiled=True),
            fc1_weight,
            preferred_element_type=jnp.float32,
        )
        + fc1_bias,
        0.0,
    ).astype(jnp.bfloat16)
    hidden_local = fc1_weight.shape[1]
    term = jnp.einsum(
        "hnf,ftc->htnc",
        active.reshape(head_count, rows_local, hidden_local),
        fc2_weight.reshape(hidden_local, tok_count, cols_local),
        preferred_element_type=jnp.float32,
    )
    down = lax.psum_scatter(
        term.reshape(head_count * tok_count * rows_local, cols_local),
        ("heads", "tok"),
        scatter_dimension=0,
        tiled=True,
    )
    hidden_out = (residual_float + down + fc2_bias).astype(jnp.bfloat16)
    return (hidden_out, appended)


def solution(mesh):
    placed = (
        P("heads", "tok"),
        P(None, None, "tok", "heads"),
        P(),
        P(),
        P(),
        P("tok", None, "heads"),
        P(None, "heads"),
        P("heads", "tok"),
        P("tok"),
        P(),
        P(),
        P(None, ("heads", "tok")),
        P(("heads", "tok")),
        P(("heads", "tok"), None),
        P("tok"),
    )
    return jax.shard_map(
        shards,
        mesh=mesh,
        in_specs=placed,
        out_specs=(P("heads", "tok"), P(None, None, "tok", "heads")),
        check_vma=False,
    )
```

profile of v0, /device:TPU:0, one launch (start us, length us, event | category | flops | bytes accessed | tf_op | source)
XLA Modules:
  0.0 1519.4 jit_solution(4574828928947439626)
XLA Ops:
  9.9 40.7 %all-reduce.1 = (f32[64]{0:T(128)S(1)}, f32[64]{0:T(128)S(1)}) all-reduce(f32[64]{0:T(128)S(1)} %get-tuple-element.71, f32[64]{0:T(128)S(1)} %get-tuple-element.70), channel_id=1, replica_groups=mesh['heads'=8,'tok'=16] {'tok'}, use_global_device_ids=true, to_apply=%region_3.0 | all-reduce | flops 128 | bytes 1024 | tf_op jit(solution)/shard_map/psum | solution.py:72
  51.6 15.4 %all_gather.27 = bf16[512,448]{1,0:T(8,128)(2,1)} all-gather(bf16[64,448]{1,0:T(8,128)(2,1)S(1)} %fusion.33), channel_id=1, replica_groups=mesh['heads'=8,'tok'=16] {'heads'}, dimensions={0}, use_global_device_ids=true | all-gather | bytes 516096 | tf_op jit(solution)/shard_map/all_gather | solution.py:78
  87.2 101.3 %all-reduce.4.cloned.1.call-done = f32[512,3,896]{0,2,1:T(8,128)} async-done(((f32[512,3,896]{0,2,1:T(8,128)}), f32[512,3,896]{0,2,1:T(8,128)}) %all-reduce.4.cloned.1.call-update) | async-done | bytes 5505040 | tf_op jit(solution)/shard_map/psum | solution.py:82
  194.0 6.1 copy.47
  204.1 6.9 gather_fusion
  211.0 6.8 gather_fusion.1
  217.8 17.6 %fusion.16 = (bf16[2,1,512,896]{3,0,2,1:T(2,128)(2,1)S(1)}, bf16[2,1,512,896]{3,0,2,1:T(2,128)(2,1)S(1)}) fusion(bf16[2,1,512,896]{3,2,1,0:T(8,128)(2,1)} %get-tuple-element.99, bf16[512,2,896]{2,1,0:T(2,128)(2,1)} %gather_fusion, pred[512]{0:T(512)(128)(4,1)S(1)} %compare_and_fusion.1, pred[512]{0:T(512)(128)(4,1)S(1)} %fusion.53, ...), kind=kLoop, calls=%fused_computation.38 | loop fusion | flops 3670016 | bytes 11012096 | tf_op jit(solution)/shard_map/stack | solution.py:93
  235.4 11.7 slice_maximum_fusion
  247.1 9.3 copy.50
  256.4 9.3 copy.51
  280.8 23.8 %all-gather.1 = f32[32,256,7]{1,2,0:T(8,128)S(1)} all-gather(f32[2,256,7]{1,2,0:T(8,128)S(1)} %get-tuple-element.109), channel_id=3, replica_groups=mesh['heads'=8,'tok'=16] {'tok'}, dimensions={0}, use_global_device_ids=true | all-gather | bytes 243712 | tf_op jit(solution)/shard_map/all_gather | solution.py:17
  310.0 22.1 %all-gather.2 = f32[32,256,7]{1,2,0:T(8,128)S(1)} all-gather(f32[2,256,7]{1,2,0:T(8,128)S(1)} %fusion.5), channel_id=4, replica_groups=mesh['heads'=8,'tok'=16] {'tok'}, dimensions={0}, use_global_device_ids=true | all-gather | bytes 243712 | tf_op jit(solution)/shard_map/all_gather | solution.py:17
  333.9 124.0 %all-gather.9.cloned.1.call-done = f32[32,256,7,128]{3,1,2,0:T(8,128)} async-done(((f32[2,256,7,128]{3,1,2,0:T(8,128)}), f32[32,256,7,128]{3,1,2,0:T(8,128)}) %all-gather.9.cloned.1.call-update) | async-done | bytes 29360144 | tf_op jit(solution)/shard_map/all_gather | solution.py:17
  461.8 20.8 %slice.86 = f32[30,256,7,128]{3,1,2,0:T(8,128)} slice(f32[32,256,7,128]{3,1,2,0:T(8,128)} %all-gather.9.cloned.1.call-done), slice={[2:32], [0:256], [0:7], [0:128]} | slice | bytes 55050240 | tf_op jit(solution)/shard_map/slice | solution.py:19
  482.6 185.3 %while.14 = (s32[]{:T(128)}, f32[2,256,7,128]{3,2,1,0:T(8,128)}, f32[2,256,7]{2,1,0:T(8,128)}, f32[2,256,7]{2,1,0:T(8,128)}, f32[15,2,256,7]{2,3,1,0:T(8,128)}, ...) while((s32[]{:T(128)}, f32[2,256,7,128]{3,2,1,0:T(8,128)}, ...), condition=%wide.region_8.10_spmd, body=%wide.region_7.9_spmd.sunk | while | flops 1397762 | bytes 18493624 | solution.py:20
  673.3 30.4 %reduce-scatter.3.cloned.1.call-done = f32[64,448]{1,0:T(8,128)} async-done(((f32[512,448]{1,0:T(8,128)}), f32[64,448]{1,0:T(8,128)}) %reduce-scatter.3.cloned.1.call-update) | async-done | bytes 114704 | tf_op jit(solution)/shard_map/reduce_scatter | solution.py:109
  704.8 40.2 %all-reduce = (f32[64]{0:T(128)S(1)}, f32[64]{0:T(128)S(1)}) all-reduce(f32[64]{0:T(128)S(1)} %get-tuple-element.69, f32[64]{0:T(128)S(1)} %get-tuple-element.68), channel_id=1, replica_groups=mesh['heads'=8,'tok'=16] {'tok'}, use_global_device_ids=true, to_apply=%region_13.15 | all-reduce | flops 128 | bytes 1024 | tf_op jit(solution)/shard_map/psum | solution.py:117
  745.1 21.6 %all-gather.3 = bf16[16,448,64]{1,2,0:T(8,128)(2,1)S(1)} all-gather(bf16[1,448,64]{1,2,0:T(8,128)(2,1)S(1)} %fusion.44), channel_id=1, replica_groups=mesh['heads'=8,'tok'=16] {'tok'}, dimensions={0}, use_global_device_ids=true | all-gather | bytes 974848 | tf_op jit(solution)/shard_map/all_gather | solution.py:123
  771.3 7.5 reshape.104
  778.8 35.7 %all-gather.7.cloned.1.call-done = bf16[512,7168]{1,0:T(8,128)(2,1)} async-done(((bf16[64,7168]{1,0:T(8,128)(2,1)}), bf16[512,7168]{1,0:T(8,128)(2,1)}) %all-gather.7.cloned.1.call-update) | async-done | bytes 7340048 | tf_op jit(solution)/shard_map/all_gather | solution.py:126
  814.5 6.1 fusion.22
  821.7 13.0 fusion.9
  834.7 7.6 pad_maximum_fusion
  844.6 666.5 %reduce-scatter.5.cloned.1.call-done = f32[64,448]{1,0:T(8,128)} async-done(((f32[8192,448]{1,0:T(8,128)}), f32[64,448]{1,0:T(8,128)}) %reduce-scatter.5.cloned.1.call-update) | async-done | bytes 114704 | tf_op jit(solution)/shard_map/reduce_scatter | solution.py:140
  (267 shorter events, 260.6 us)
Async XLA Ops:
  7.2 807.3 %copy-start = (bf16[7168,224]{0,1:T(8,128)(2,1)S(1)}, bf16[7168,224]{0,1:T(8,128)(2,1)}, u32[]{:S(2)}) copy-start(bf16[7168,224]{0,1:T(8,128)(2,1)} %param.31) | copy-start | bytes 9633796
  7.2 181.4 %all-reduce.4.cloned.1.call-start = ((), (), s32[]{:S(2)}) async-start(), calls=%async_computation.2 | async-start | bytes 11010048 | tf_op jit(solution)/shard_map/psum | solution.py:82
  77.3 380.6 %all-gather.9.cloned.1.call-start = ((), (), s32[]{:S(2)}) async-start(), calls=%async_computation.6 | async-start | bytes 31195136 | tf_op jit(solution)/shard_map/all_gather | solution.py:17
  82.9 105.6 %copy-start.9 = (f32[3,896]{1,0:T(4,128)S(1)}, f32[3,896]{1,0:T(4,128)}, u32[]{:S(2)}) copy-start(f32[3,896]{1,0:T(4,128)} %param.26) | copy-start | bytes 32260
  83.0 105.6 %copy-start.13 = (f32[3]{0:T(128)S(1)}, f32[3]{0:T(128)}, u32[]{:S(2)}) copy-start(f32[3]{0:T(128)} %constant.59.clone) | copy-start | bytes 40
  235.4 11.7 copy-start.3
  235.4 11.7 copy-start.4
  268.8 6.2 copy-start.5
  280.8 422.9 %reduce-scatter.3.cloned.1.call-start = ((), (), s32[]{:S(2)}) async-start(), calls=%async_computation.3 | async-start | bytes 1179648 | tf_op jit(solution)/shard_map/reduce_scatter | solution.py:109
  489.5 5.4 copy-start.8
  501.9 5.4 copy-start.8
  526.6 5.4 copy-start.8
  539.0 5.4 copy-start.8
  551.3 5.4 copy-start.8
  576.0 5.4 copy-start.8
  588.4 5.4 copy-start.8
  600.7 5.4 copy-start.8
  625.4 5.4 copy-start.8
  670.0 33.8 %copy-start.6 = (bf16[64,448]{1,0:T(8,128)(2,1)S(1)}, bf16[64,448]{1,0:T(8,128)(2,1)}, u32[]{:S(2)}) copy-start(bf16[64,448]{1,0:T(8,128)(2,1)} %param.20) | copy-start | bytes 172036
  670.0 33.8 %copy-start.11 = (f32[448]{0:T(512)S(1)}, f32[448]{0:T(512)}, u32[]{:S(2)}) copy-start(f32[448]{0:T(512)} %param.28) | copy-start | bytes 5380
  671.7 142.8 %all-gather.7.cloned.1.call-start = ((), (), s32[]{:S(2)}) async-start(), calls=%async_computation.4 | async-start | bytes 8257536 | tf_op jit(solution)/shard_map/all_gather | solution.py:126
  771.2 43.2 %copy-start.15 = (f32[224]{0:T(256)S(1)}, f32[224]{0:T(256)}, u32[]{:S(2)}) copy-start(f32[224]{0:T(256)} %param.32) | copy-start | bytes 2692
  771.3 739.8 %reduce-scatter.5.cloned.1.call-start = ((), (), s32[]{:S(2)}) async-start(), calls=%async_computation.5 | async-start | bytes 16908288 | tf_op jit(solution)/shard_map/reduce_scatter | solution.py:140
  842.3 668.8 %copy-start.12 = (f32[448]{0:T(512)S(1)}, f32[448]{0:T(512)}, u32[]{:S(2)}) copy-start(f32[448]{0:T(512)} %param.34) | copy-start | bytes 5380
  (40 other events, 127.9 us)
Sparse Core Ops, SparseCore 0:
  77.5 111.0 all-reduce.3
  280.9 176.9 all-gather.8
  671.8 31.8 reduce-scatter.2
  771.4 43.0 all-gather.6
  834.8 676.2 reduce-scatter.4
where the time goes:
time: 1530 us; the launch traced here: 1520 us
  waiting for transfers between devices  958 us (63%)
  local copies, waits for them, and re-layouts  181 us (12%)
  other arithmetic  169 us (11%)
  blocking collectives  164 us (11%)
  matrix products  33 us (2%)
    reduce_scatter x1, waiting for transfers between devices, shards(): lax.psum_scatter(term.reshape(head_count * tok_count * rows_local, cols_l...  667 us
    all_gather x1, waiting for transfers between devices, joined(): pieces = jax.tree.map(lambda part: lax.all_gather(part, axis), value)  124 us
    psum x1, waiting for transfers between devices, shards(): summed = lax.psum(partial_qkv, 'tok')  101 us
    add x15, other arithmetic, merge_parts(): first[0] * left_factor[..., None] + second[0] * right_factor[..., None]  81.5 us
    dynamic_slice x60, local copies, waits for them, and re-layouts, joined(): lax.scan(lambda so_far, section: (join(so_far, section), None), head, tail)  71.5 us
    all_gather x2, blocking collectives, joined(): pieces = jax.tree.map(lambda part: lax.all_gather(part, axis), value)  45.9 us
    psum x1, blocking collectives, shards(): lax.psum((jnp.sum(states_float, axis=1), jnp.sum(states_float * states_fl...  40.7 us
    psum x1, blocking collectives, shards(): lax.psum((jnp.sum(residual_float, axis=1), jnp.sum(residual_float * resid...  40.2 us
  transfers between devices with their start and end apart: 5, of which 5 were waited for; matrix products, arithmetic and copies ran while one was open for 2% of the time, Pallas kernels for 0%

commit v1 on v0

--- a/solution.py
+++ b/solution.py
@@ -13,31 +13,12 @@
 NEGATIVE = -1e30
 
 
-def joined(value, axis, join):
-    pieces = jax.tree.map(lambda part: lax.all_gather(part, axis), value)
-    head = jax.tree.map(lambda part: part[0], pieces)
-    tail = jax.tree.map(lambda part: part[1:], pieces)
-    so_far, _ = lax.scan(lambda so_far, section: (join(so_far, section), None), head, tail)
-    return so_far
-
-
 def norm_rows(values, total_sum, total_square, width, gain, shift):
     mean_row = total_sum / width
     variance = total_square / width - mean_row * mean_row
     return (
         (values - mean_row[:, None]) * lax.rsqrt(variance[:, None] + EPSILON) * gain + shift
     ).astype(jnp.bfloat16)
-
-
-def merge_parts(first, second):
-    highest = jnp.maximum(first[1], second[1])
-    left_factor = jnp.exp(first[1] - highest)
-    right_factor = jnp.exp(second[1] - highest)
-    return (
-        first[0] * left_factor[..., None] + second[0] * right_factor[..., None],
-        highest,
-        first[2] * left_factor + second[2] * right_factor,
-    )
 
 
 def shards(
@@ -79,8 +60,9 @@
     weight_flat = qkv_weight.reshape(cols_local, 3 * group)
     factors = jnp.asarray([HD ** (-0.5), 1.0, 1.0], dtype=jnp.float32)[None, :, None]
     partial_qkv = jnp.dot(gathered, weight_flat, preferred_element_type=jnp.float32)
-    summed = lax.psum(partial_qkv, "tok")
-    projected = ((summed.reshape(tokens, 3, group) + qkv_bias[None]) * factors).astype(jnp.bfloat16)
+    summed = lax.psum_scatter(partial_qkv, "tok", scatter_dimension=0, tiled=True)
+    projected_part = ((summed.reshape(-1, 3, group) + qkv_bias[None]) * factors).astype(jnp.bfloat16)
+    projected = lax.all_gather(projected_part, "tok", axis=0, tiled=True)
     queries = projected[:, 0].reshape(REQS, NEW, group_heads, HD)
     fresh = jnp.moveaxis(projected[:, 1:].reshape(REQS, NEW, 2, group), 2, 0)
     key_pos = tok_index * cache_rows + jnp.arange(cache_rows, dtype=jnp.int32)
@@ -98,14 +80,18 @@
     allowed = (distance >= 0) & ((key_pos[None, None, :] < SINK) | (distance < window))
     scores = jnp.einsum("rshd,rphd->rshp", queries, keys, preferred_element_type=jnp.float32)
     masked = jnp.where(allowed[:, :, None, :], scores, NEGATIVE)
-    peak = jnp.max(masked, axis=-1)
+    peak = lax.pmax(jnp.max(masked, axis=-1), "tok")
     weights = jnp.where(allowed[:, :, None, :], jnp.exp(masked - peak[..., None]), 0.0)
     totals = jnp.sum(weights, axis=-1)
     partial_out = jnp.einsum(
         "rshp,rphd->rshd", weights.astype(jnp.bfloat16), values, preferred_element_type=jnp.float32
     )
-    merged, highest, denominator = joined((partial_out, peak, totals), "tok", merge_parts)
-    attended = (merged / denominator[..., None]).astype(jnp.bfloat16).reshape(tokens, group)
+    merged = lax.psum_scatter(partial_out.reshape(tokens, group), "tok", scatter_dimension=0, tiled=True)
+    denominator = lax.psum_scatter(totals.reshape(tokens, group_heads), "tok", scatter_dimension=0, tiled=True)
+    attended_part = (
+        (merged.reshape(-1, group_heads, HD) / denominator[..., None]).astype(jnp.bfloat16).reshape(-1, group)
+    )
+    attended = lax.all_gather(attended_part, "tok", axis=0, tiled=True)
     projected_out = lax.psum_scatter(
         jnp.dot(attended, out_weight, preferred_element_type=jnp.float32),
         "heads",
@@ -137,12 +123,14 @@
         fc2_weight.reshape(hidden_local, tok_count, cols_local),
         preferred_element_type=jnp.float32,
     )
-    down = lax.psum_scatter(
-        term.reshape(head_count * tok_count * rows_local, cols_local),
+    pieces = lax.all_to_all(
+        term.reshape(head_count * tok_count, rows_local, cols_local).astype(jnp.bfloat16),
         ("heads", "tok"),
-        scatter_dimension=0,
+        0,
+        0,
         tiled=True,
     )
+    down = jnp.sum(pieces.astype(jnp.float32), axis=0)
     hidden_out = (residual_float + down + fc2_bias).astype(jnp.bfloat16)
     return (hidden_out, appended)
 

time: 1530 us -> 827 us (0.54)
  the two profiles are of different devices: /device:TPU:0 before, /device:TPU:5 now
where the time goes in v1:
time: 827 us; the launch traced here: 820 us
  waiting for transfers between devices  447 us (54%)
  blocking collectives  174 us (21%)
  local copies, waits for them, and re-layouts  80.5 us (10%)
  other arithmetic  56.6 us (7%)
  matrix products  38.2 us (5%)
  between operations  14.5 us (2%)
  starting transfers between devices  9.09 us (1%)
    all_to_all x1, waiting for transfers between devices, shards(): lax.all_to_all(term.reshape(head_count * tok_count, rows_local, cols_loca...  96.7 us
    reduce_scatter x1, waiting for transfers between devices, shards(): lax.psum_scatter(partial_qkv, 'tok', scatter_dimension=0, tiled=True)  77.9 us
    reduce_scatter x1, waiting for transfers between devices, shards(): lax.psum_scatter(partial_out.reshape(tokens, group), 'tok', scatter_dimen...  76.7 us
    reduce_scatter x1, waiting for transfers between devices, shards(): lax.psum_scatter(totals.reshape(tokens, group_heads), 'tok', scatter_dime...  71.3 us
    pmax x1, blocking collectives, shards(): peak = lax.pmax(jnp.max(masked, axis=-1), 'tok')  55.4 us
    all_gather x1, waiting for transfers between devices, shards(): lax.all_gather(normed, 'heads', axis=0, tiled=True)  52.3 us
    another operation x3, other arithmetic, shards(): appended = jnp.stack(appended_parts, axis=1)  36.8 us
    all_gather x1, waiting for transfers between devices, shards(): projected = lax.all_gather(projected_part, 'tok', axis=0, tiled=True)  36.4 us
  transfers between devices with their start and end apart: 7, of which 7 were waited for; matrix products, arithmetic and copies ran while one was open for 5% of the time, Pallas kernels for 0%

profile of v1, /device:TPU:5, one launch (start us, length us, event | category | flops | bytes accessed | tf_op | source)
XLA Modules:
  0.0 819.8 jit_solution(16059058583653512744)
XLA Ops:
  9.9 29.1 %all-reduce.1 = (f32[64]{0:T(128)S(1)}, f32[64]{0:T(128)S(1)}) all-reduce(f32[64]{0:T(128)S(1)} %get-tuple-element.14, f32[64]{0:T(128)S(1)} %get-tuple-element.13), channel_id=1, replica_groups=mesh['heads'=8,'tok'=16] {'tok'}, use_global_device_ids=true, to_apply=%region_3.0 | all-reduce | flops 128 | bytes 1024 | tf_op jit(solution)/shard_map/psum | solution.py:53
  40.0 23.1 %all_gather.15 = bf16[512,448]{1,0:T(8,128)(2,1)} all-gather(bf16[64,448]{1,0:T(8,128)(2,1)S(1)} %fusion.25), channel_id=1, replica_groups=mesh['heads'=8,'tok'=16] {'heads'}, dimensions={0}, use_global_device_ids=true | all-gather | bytes 516096 | tf_op jit(solution)/shard_map/all_gather | solution.py:59
  73.6 77.9 %reduce-scatter.9.cloned.1.call-done = f32[32,2688]{1,0:T(8,128)} async-done(((f32[512,2688]{1,0:T(8,128)}), f32[32,2688]{1,0:T(8,128)}) %reduce-scatter.9.cloned.1.call-update) | async-done | bytes 344080 | tf_op jit(solution)/shard_map/reduce_scatter | solution.py:63
  164.6 36.4 %all-gather.4.cloned.1.call-done = bf16[512,3,896]{2,0,1:T(8,128)(2,1)} async-done(((bf16[32,3,896]{2,0,1:T(8,128)(2,1)}), bf16[512,3,896]{2,0,1:T(8,128)(2,1)}) %all-gather.4.cloned.1.call-update) | async-done | bytes 2752528 | tf_op jit(solution)/shard_map/all_gather | solution.py:65
  211.0 6.8 gather_fusion
  217.8 6.8 gather_fusion.1
  224.6 17.6 %fusion.11 = (bf16[2,1,512,896]{3,0,2,1:T(2,128)(2,1)S(1)}, bf16[2,1,512,896]{3,0,2,1:T(2,128)(2,1)S(1)}) fusion(bf16[2,1,512,896]{3,2,1,0:T(8,128)(2,1)} %get-tuple-element.22, bf16[512,2,896]{2,1,0:T(2,128)(2,1)} %gather_fusion, pred[512]{0:T(512)(128)(4,1)S(1)} %compare_and_fusion.1, pred[512]{0:T(512)(128)(4,1)S(1)} %fusion.46, ...), kind=kLoop, calls=%fused_computation.26 | loop fusion | flops 3670016 | bytes 11012096 | tf_op jit(solution)/shard_map/stack | solution.py:75
  242.2 11.7 %slice_maximum_fusion = (bf16[1,2,512,896]{3,0,2,1:T(2,128)(2,1)}, bf16[1,2,512,896]{3,0,2,1:T(2,128)(2,1)}) fusion(bf16[2,1,512,896]{3,0,2,1:T(2,128)(2,1)S(1)} %get-tuple-element.35, bf16[2,1,512,896]{3,0,2,1:T(2,128)(2,1)S(1)} %get-tuple-element.34), kind=kLoop, calls=%fused_computation.10 | loop fusion | flops 1835008 | bytes 7340032 | tf_op jit(solution)/shard_map/stack | solution.py:75
  254.0 9.3 %copy.80 = bf16[1,2,512,896]{2,3,1,0:T(8,128)(2,1)} copy(bf16[1,2,512,896]{3,0,2,1:T(2,128)(2,1)} %get-tuple-element.20) | data formatting | bytes 3670016 | tf_op jit(solution)/shard_map/slice | solution.py:76
  263.3 9.3 %copy.79 = bf16[1,2,512,896]{2,3,1,0:T(8,128)(2,1)} copy(bf16[1,2,512,896]{3,0,2,1:T(2,128)(2,1)} %get-tuple-element.21) | data formatting | bytes 3670016 | tf_op jit(solution)/shard_map/slice | solution.py:77
  278.7 55.4 %pmax.7 = f32[2,256,7]{1,2,0:T(8,128)S(1)} all-reduce(f32[2,256,7]{1,2,0:T(8,128)S(1)} %get-tuple-element.32), channel_id=1, replica_groups=mesh['heads'=8,'tok'=16] {'tok'}, use_global_device_ids=true, to_apply=%region_6.8 | all-reduce | flops 3584 | bytes 28672 | tf_op jit(solution)/shard_map/pmax | solution.py:83
  339.7 6.7 fusion.13
  352.6 71.3 %reduce-scatter.15.cloned.1.call-done = f32[32,7]{1,0:T(8,128)} async-done(((f32[512,7]{1,0:T(8,128)}), f32[32,7]{1,0:T(8,128)}) %reduce-scatter.15.cloned.1.call-update) | async-done | bytes 912 | tf_op jit(solution)/shard_map/reduce_scatter | solution.py:90
  423.9 76.7 %reduce-scatter.13.cloned.1.call-done = f32[32,896]{1,0:T(8,128)} async-done(((f32[512,896]{1,0:T(8,128)}), f32[32,896]{1,0:T(8,128)}) %reduce-scatter.13.cloned.1.call-update) | async-done | bytes 114704 | tf_op jit(solution)/shard_map/reduce_scatter | solution.py:89
  502.4 17.8 %all_gather.17 = bf16[512,896]{1,0:T(8,128)(2,1)S(1)} all-gather(bf16[32,896]{1,0:T(8,128)(2,1)S(1)} %fusion.36), channel_id=1, replica_groups=mesh['heads'=8,'tok'=16] {'tok'}, dimensions={0}, use_global_device_ids=true | all-gather | bytes 974848 | tf_op jit(solution)/shard_map/all_gather | solution.py:94
  524.6 35.3 %reduce-scatter.11.cloned.1.call-done = f32[64,448]{1,0:T(8,128)} async-done(((f32[512,448]{1,0:T(8,128)}), f32[64,448]{1,0:T(8,128)}) %reduce-scatter.11.cloned.1.call-update) | async-done | bytes 114704 | tf_op jit(solution)/shard_map/reduce_scatter | solution.py:95
  561.0 29.0 %all-reduce = (f32[64]{0:T(128)S(1)}, f32[64]{0:T(128)S(1)}) all-reduce(f32[64]{0:T(128)S(1)} %get-tuple-element.12, f32[64]{0:T(128)S(1)} %get-tuple-element.11), channel_id=1, replica_groups=mesh['heads'=8,'tok'=16] {'tok'}, use_global_device_ids=true, to_apply=%region_14.16 | all-reduce | flops 128 | bytes 1024 | tf_op jit(solution)/shard_map/psum | solution.py:103
  590.1 19.8 %all-gather = bf16[16,448,64]{1,2,0:T(8,128)(2,1)S(1)} all-gather(bf16[1,448,64]{1,2,0:T(8,128)(2,1)S(1)} %fusion.37), channel_id=1, replica_groups=mesh['heads'=8,'tok'=16] {'tok'}, dimensions={0}, use_global_device_ids=true | all-gather | bytes 974848 | tf_op jit(solution)/shard_map/all_gather | solution.py:109
  614.7 7.3 reshape.108
  622.0 52.3 %all-gather.6.cloned.1.call-done = bf16[512,7168]{1,0:T(8,128)(2,1)} async-done(((bf16[64,7168]{1,0:T(8,128)(2,1)}), bf16[512,7168]{1,0:T(8,128)(2,1)}) %all-gather.6.cloned.1.call-update) | async-done | bytes 7340048 | tf_op jit(solution)/shard_map/all_gather | solution.py:112
  681.5 10.4 %convolution_convert_fusion = bf16[8,64,16,448]{3,1,2,0:T(8,128)(2,1)} fusion(bf16[8,64,224,1]{2,1,3,0:T(8,128)(2,1)S(1)} %bitcast.101, bf16[224,16,448]{2,1,0:T(8,128)(2,1)} %reshape.108), kind=kOutput, calls=%fused_computation.5 | convolution fusion | flops 1647837184 | bytes 10780672 | tf_op jit(solution)/shard_map/hnf,ftc->htnc/dot_general | solution.py:120
  691.9 8.8 %all-to-all-start = ((bf16[128,64,448]{2,1,0:T(8,128)(2,1)}), bf16[128,64,448]{2,1,0:T(8,128)(2,1)}, u32[]{:S(2)}, u32[]{:S(2)}) async-start(bf16[128,64,448]{2,1,0:T(8,128)(2,1)} %bitcast.93), calls=%async_computation.2 | async-start | bytes 16777216 | tf_op jit(solution)/shard_map/all_to_all | solution.py:126
  700.7 7.6 pad_maximum_fusion
  710.6 96.7 %all-to-all-done = bf16[128,64,448]{2,1,0:T(8,128)(2,1)} async-done(((bf16[128,64,448]{2,1,0:T(8,128)(2,1)}), bf16[128,64,448]{2,1,0:T(8,128)(2,1)}, u32[]{:S(2)}, u32[]{:S(2)}) %all-to-all-start) | async-done | bytes 7340064 | tf_op jit(solution)/shard_map/all_to_all | solution.py:126
  (84 shorter events, 82.0 us)
Async XLA Ops:
  7.2 667.1 %copy-start = (bf16[7168,224]{0,1:T(8,128)(2,1)S(1)}, bf16[7168,224]{0,1:T(8,128)(2,1)}, u32[]{:S(2)}) copy-start(bf16[7168,224]{0,1:T(8,128)(2,1)} %param.29) | copy-start | bytes 9633796
  7.2 144.3 %reduce-scatter.9.cloned.1.call-start = ((), (), s32[]{:S(2)}) async-start(), calls=%async_computation.5 | async-start | bytes 5849088 | tf_op jit(solution)/shard_map/reduce_scatter | solution.py:63
  73.5 79.9 %copy-start.5 = (f32[3,896]{1,0:T(4,128)S(1)}, f32[3,896]{1,0:T(4,128)}, u32[]{:S(2)}) copy-start(f32[3,896]{1,0:T(4,128)} %param.24) | copy-start | bytes 32260
  73.5 79.9 %copy-start.9 = (f32[3]{0:T(128)S(1)}, f32[3]{0:T(128)}, u32[]{:S(2)}) copy-start(f32[3]{0:T(128)} %constant.22.clone) | copy-start | bytes 40
  73.5 81.8 %copy-start.6 = (s32[2]{0:T(128)S(1)}, s32[2]{0:T(128)}, u32[]{:S(2)}) copy-start(s32[2]{0:T(128)} %param.20) | copy-start | bytes 28
  73.5 127.4 %all-gather.4.cloned.1.call-start = ((), (), s32[]{:S(2)}) async-start(), calls=%async_computation.6 | async-start | bytes 2924544 | tf_op jit(solution)/shard_map/all_gather | solution.py:65
  155.3 268.7 %reduce-scatter.15.cloned.1.call-start = ((), (), s32[]{:S(2)}) async-start(), calls=%async_computation.10 | async-start | bytes 278528 | tf_op jit(solution)/shard_map/reduce_scatter | solution.py:90
  201.0 1.5 slice-start
  202.5 4.4 copy-start.3
  242.2 11.8 %copy-start.1 = (bf16[2,1,512,896]{3,0,2,1:T(2,128)(2,1)}, bf16[2,1,512,896]{3,0,2,1:T(2,128)(2,1)S(1)}, u32[]{:S(2)}) copy-start(bf16[2,1,512,896]{3,0,2,1:T(2,128)(2,1)S(1)} %get-tuple-element.34) | copy-start | bytes 5505028
  242.2 11.7 %copy-start.2 = (bf16[2,1,512,896]{3,0,2,1:T(2,128)(2,1)}, bf16[2,1,512,896]{3,0,2,1:T(2,128)(2,1)S(1)}, u32[]{:S(2)}) copy-start(bf16[2,1,512,896]{3,0,2,1:T(2,128)(2,1)S(1)} %get-tuple-element.35) | copy-start | bytes 5505028
  339.7 161.0 %reduce-scatter.13.cloned.1.call-start = ((), (), s32[]{:S(2)}) async-start(), calls=%async_computation.9 | async-start | bytes 1949696 | tf_op jit(solution)/shard_map/reduce_scatter | solution.py:89
  352.6 207.4 %copy-start.4 = (bf16[64,448]{1,0:T(8,128)(2,1)S(1)}, bf16[64,448]{1,0:T(8,128)(2,1)}, u32[]{:S(2)}) copy-start(bf16[64,448]{1,0:T(8,128)(2,1)} %param.18) | copy-start | bytes 172036
  352.6 207.4 %copy-start.7 = (f32[448]{0:T(512)S(1)}, f32[448]{0:T(512)}, u32[]{:S(2)}) copy-start(f32[448]{0:T(512)} %param.26) | copy-start | bytes 5380
  352.6 207.3 %reduce-scatter.11.cloned.1.call-start = ((), (), s32[]{:S(2)}) async-start(), calls=%async_computation.7 | async-start | bytes 1179648 | tf_op jit(solution)/shard_map/reduce_scatter | solution.py:95
  523.0 151.3 %all-gather.6.cloned.1.call-start = ((), (), s32[]{:S(2)}) async-start(), calls=%async_computation.8 | async-start | bytes 8257536 | tf_op jit(solution)/shard_map/all_gather | solution.py:112
  614.7 59.6 %copy-start.10 = (f32[224]{0:T(256)S(1)}, f32[224]{0:T(256)}, u32[]{:S(2)}) copy-start(f32[224]{0:T(256)} %param.30) | copy-start | bytes 2692
  691.9 115.4 %all-to-all-start = ((bf16[128,64,448]{2,1,0:T(8,128)(2,1)}), bf16[128,64,448]{2,1,0:T(8,128)(2,1)}, u32[]{:S(2)}, u32[]{:S(2)}) async-start(bf16[128,64,448]{2,1,0:T(8,128)(2,1)} %bitcast.93), calls=%async_computation.2 | async-start | bytes 16777216 | tf_op jit(solution)/shard_map/all_to_all | solution.py:126
  710.6 101.5 %copy-start.8 = (f32[448]{0:T(512)S(1)}, f32[448]{0:T(512)}, u32[]{:S(2)}) copy-start(f32[448]{0:T(512)} %param.32) | copy-start | bytes 5380
Sparse Core Ops, SparseCore 0:
  73.6 77.7 reduce-scatter.8
  155.4 45.5 all-gather.3
  339.8 84.1 reduce-scatter.14
  427.4 73.2 reduce-scatter.12
  523.1 36.7 reduce-scatter.10
  614.8 59.4 all-gather.5
